TPU v7x, 256 devices: a whole 4x4x8 slice. The times are simulated.
256 devices in a mesh: row: 16 (over x, y_hi, core), col: 16 (over y_lo, z).
Axes of the slice: x: 4, y: 4 (y_hi: 2, y_lo: 2; y = y_hi * 2 + y_lo), z: 8, core: 2. Of those that a mesh axis runs over, the one named last changes fastest.
Arguments:
- query_in: bfloat16 [4096, 8192], P('row', 'col'), may hold values from -6 to 6
- key_in: bfloat16 [4096, 8192], P('row', 'col'), may hold values from -6 to 6
- value_in: bfloat16 [4096, 8192], P('row', 'col'), may hold values from -6 to 6
- filters: float32 [512, 128], P('col'), may hold values from -0.5 to 0.5
- out_weight: bfloat16 [8192, 8192], P('row', 'col'), may hold values from -0.0625 to 0.0625
- out_grad: bfloat16 [4096, 8192], P('row', 'col'), may hold values from -6 to 6
Outputs:
- mixed: bfloat16 [4096, 8192], P('row', 'col')
- query_grad: bfloat16 [4096, 8192], P('row', 'col')
- key_grad: bfloat16 [4096, 8192], P('row', 'col')
- value_grad: bfloat16 [4096, 8192], P('row', 'col')
- weight_grad: bfloat16 [8192, 8192], P('row', 'col')
- filter_grad: float32 [512, 128], P('col')
All inputs are finite; a program needn't handle non-finite values.
Results may differ from a plain program's by a relative error of at most 0.018.
Values may be sent and summed in bfloat16 or wider, within the bound.
A program may use at most 128 MiB of HBM per device.

v0:
```python
import math
import jax
import jax.numpy as jnp
from jax import lax
from jax.sharding import PartitionSpec as P


def from_behind(shard, axis, by):
    size = lax.axis_size(axis)
    pairs = [(i, i + by) for i in range(size) if 0 <= i + by < size]
    return lax.ppermute(shard, axis, pairs)


def toeplitz(taps, causal):
    groups, span = taps.shape
    if causal:
        template = jnp.concatenate(
            [
                jnp.zeros((groups, 1), jnp.float32),
                taps[:, ::-1],
                jnp.zeros((groups, span), jnp.float32),
            ],
            1,
        )
    else:
        template = jnp.concatenate([taps, jnp.zeros((groups, span + 1), jnp.float32)], 1)
    tiled = jnp.tile(template, (1, span))
    return tiled[:, : 2 * span * span].reshape(groups, span, 2 * span)


def windows(extended, span):
    count = (extended.shape[0] - span) // span
    first = extended[:-span].reshape(count, span, extended.shape[1])
    second = extended[span:].reshape(count, span, extended.shape[1])
    return jnp.concatenate([first, second], axis=1)


def convolve(matrix, extended, span, group):
    blocks = windows(extended, span)
    count, _, width = blocks.shape
    split = blocks.reshape(count, 2 * span, width // group, group)
    result = jnp.einsum("gts,bsgc->btgc", matrix, split, precision=lax.Precision.HIGHEST)
    return result.reshape(count * span, width)


def shards(query_in, key_in, value_in, filters, out_weight, out_grad):
    f32 = jnp.float32
    bf16 = jnp.bfloat16
    tokens, width = query_in.shape
    span = filters.shape[1]
    group = width // filters.shape[0]
    total_tokens = tokens * lax.axis_size("row")
    key32 = key_in.astype(f32)
    value32 = value_in.astype(f32)
    query32 = query_in.astype(f32)
    product = key32 * value32
    key_rim, value_rim = from_behind((key_in[-span:], value_in[-span:]), "row", 1)
    product_rim = key_rim.astype(f32) * value_rim.astype(f32)
    product_ext = jnp.concatenate([product_rim, product], 0)
    conv = convolve(toeplitz(filters, True), product_ext, span, group)
    gated = (query32 * conv).astype(bf16)
    panel = lax.all_gather(gated, "col", axis=1, tiled=True)
    weights = lax.all_gather(out_weight, "row", axis=0, tiled=True)
    mixed_sum = jnp.dot(panel, weights, preferred_element_type=f32)
    partial_value = lax.dot_general(
        out_grad, weights, (((1,), (1,)), ((), ())), preferred_element_type=f32
    )
    mixed = mixed_sum.astype(bf16)
    grad_gated = lax.psum_scatter(
        partial_value.astype(jnp.bfloat16), "col", scatter_dimension=1, tiled=True
    ).astype(jnp.float32)
    query_grad = (grad_gated * conv).astype(bf16)
    grad_conv = grad_gated * query32
    grad_rim = from_behind(grad_conv[:span].astype(jnp.bfloat16), "row", -1).astype(jnp.float32)
    grad_ext = jnp.concatenate([grad_conv, grad_rim], 0)
    grad_product = convolve(toeplitz(filters, False), grad_ext, span, group)
    key_grad = (grad_product * value32).astype(bf16)
    value_grad = (grad_product * key32).astype(bf16)
    count = tokens // span
    groups = width // group
    grad_blocks = grad_conv.reshape(count, span, groups, group)
    product_blocks = windows(product_ext, span).reshape(count, 2 * span, groups, group)
    corr = jnp.einsum(
        "btgc,bsgc->gts", grad_blocks, product_blocks, precision=lax.Precision.HIGHEST
    )
    flat = jnp.concatenate(
        [corr.reshape(groups, 2 * span * span), jnp.zeros((groups, span), f32)], 1
    )
    skewed = flat.reshape(groups, span, 2 * span + 1)[:, :, 1 : span + 1]
    local_taps = jnp.sum(skewed, axis=1)[:, ::-1]
    filter_grad = lax.psum(local_taps, "row") * (1.0 / math.sqrt(total_tokens * group))
    weight_sum = lax.psum_scatter(
        lax.dot_general(
            panel, out_grad, (((0,), (0,)), ((), ())), preferred_element_type=f32
        ).astype(jnp.bfloat16),
        "row",
        scatter_dimension=0,
        tiled=True,
    ).astype(jnp.float32)
    weight_grad = (weight_sum * (1.0 / math.sqrt(total_tokens))).astype(bf16)
    return (mixed, query_grad, key_grad, value_grad, weight_grad, filter_grad)


def solution(mesh):
    placed = (
        P("row", "col"),
        P("row", "col"),
        P("row", "col"),
        P("col", None),
        P("row", "col"),
        P("row", "col"),
    )
    return jax.shard_map(
        shards,
        mesh=mesh,
        in_specs=placed,
        out_specs=(
            P("row", "col"),
            P("row", "col"),
            P("row", "col"),
            P("row", "col"),
            P("row", "col"),
            P("col", None),
        ),
        check_vma=False,
    )
```

profile of v0, /device:TPU:2, one launch (start us, length us, event | category | flops | bytes accessed | tf_op | source)
XLA Modules:
  0.0 399.6 jit_solution(14120310710008545654)
XLA Ops:
  8.0 82.3 %all-gather.5.cloned.1.call-done = bf16[8192,512]{1,0:T(8,128)(2,1)} async-done(((bf16[512,512]{1,0:T(8,128)(2,1)}), bf16[8192,512]{1,0:T(8,128)(2,1)}) %all-gather.5.cloned.1.call-update) | async-done | bytes 8388624 | tf_op jit(solution)/shard_map/all_gather | solution.py:63
  90.2 7.8 %convolution_convert_fusion.1 = bf16[256,8192]{1,0:T(8,128)(2,1)} fusion(bf16[256,512]{1,0:T(8,128)(2,1)S(1)} %copy-done, bf16[8192,512]{1,0:T(8,128)(2,1)} %all-gather.5.cloned.1.call-done), kind=kOutput, calls=%fused_computation.1 | convolution fusion | flops 2149580800 | bytes 12845056 | tf_op jit(solution)/shard_map/dot_general | solution.py:65
  98.1 0.9 copy-done.6
  99.2 2.1 collective-permute-start
  101.5 2.3 collective-permute-start.1
  103.9 3.1 tile.20
  107.0 6.7 %tile.21 = f32[32,32896]{1,0:T(8,128)} reshape(f32[32,128,257]{2,1,0:T(8,128)} %tile.20) | data formatting | bytes 8421376 | tf_op jit(solution)/shard_map/tile | solution.py:27
  113.7 2.2 slice-done
  115.9 3.3 copy.37
  119.4 3.1 tile.8
  122.5 6.7 %tile.9 = f32[32,32896]{1,0:T(8,128)} reshape(f32[32,128,257]{2,1,0:T(8,128)} %tile.8) | data formatting | bytes 8421376 | tf_op jit(solution)/shard_map/tile | solution.py:27
  129.2 2.2 slice-done.1
  131.4 3.2 copy.35
  134.6 44.5 %reduce-scatter.3.cloned.1.call-done = bf16[256,512]{1,0:T(8,128)(2,1)} async-done(((bf16[256,8192]{1,0:T(8,128)(2,1)}), bf16[256,512]{1,0:T(8,128)(2,1)}) %reduce-scatter.3.cloned.1.call-update) | async-done | bytes 262160 | tf_op jit(solution)/shard_map/reduce_scatter | solution.py:69
  179.1 1.0 convert_multiply_fusion
  180.8 2.1 collective-permute-start.2
  183.5 2.0 collective-permute-done.2
  186.2 5.9 %fusion.7 = f32[2,128,32,16]{1,3,0,2:T(8,128)S(1)} fusion(f32[32,128,256,1]{2,1,0,3:T(8,128)} %bitcast.60, f32[2,128,32,16]{1,3,0,2:T(8,128)S(1)} %copy.27, f32[2,128,32,16]{1,3,0,2:T(8,128)S(1)} %copy.26), kind=kOutput, calls=%fused_computation.8 | convolution fusion | flops 402915328 | bytes 5767168 | tf_op jit(solution)/shard_map/gts,bsgc->btgc/dot_general | solution.py:42
  192.4 0.9 fusion.14
  194.0 5.9 %fusion.4 = f32[2,128,32,16]{1,3,0,2:T(8,128)S(1)} fusion(f32[2,256,32,16]{1,3,0,2:T(8,128)S(1)} %copy_dynamic-update-slice_fusion, f32[32,128,256,1]{2,1,0,3:T(8,128)} %bitcast.59), kind=kOutput, calls=%fused_computation.7 | convolution fusion | flops 402653184 | bytes 5767168 | tf_op jit(solution)/shard_map/gts,bsgc->btgc/dot_general | solution.py:42
  200.5 0.9 fusion.16
  201.7 73.7 %all-gather.3.cloned.1.call-done = bf16[256,8192]{1,0:T(8,128)(2,1)} async-done(((bf16[256,512]{1,0:T(8,128)(2,1)}), bf16[256,8192]{1,0:T(8,128)(2,1)}) %all-gather.3.cloned.1.call-update) | async-done | bytes 4194320 | tf_op jit(solution)/shard_map/all_gather | solution.py:62
  275.4 7.8 %convolution_convert_fusion = bf16[8192,512]{1,0:T(8,128)(2,1)} fusion(bf16[256,8192]{1,0:T(8,128)(2,1)} %all-gather.3.cloned.1.call-done, bf16[256,512]{1,0:T(8,128)(2,1)S(1)} %copy-done), kind=kOutput, calls=%fused_computation | convolution fusion | flops 2151677952 | bytes 12845056 | tf_op jit(solution)/shard_map/dot_general | solution.py:93
  283.2 3.5 fusion.18
  286.7 2.4 copy.39
  289.2 2.3 concatenate.42
  291.5 8.2 %reshape.61 = f32[32,128,257]{2,1,0:T(8,128)} reshape(f32[32,32896]{1,0:T(8,128)} %concatenate.42) | data formatting | bytes 8421376 | tf_op jit(solution)/shard_map/reshape | solution.py:89
  299.7 3.2 slice_reduce_fusion
  304.7 57.5 %psum.7 = f32[32,128]{1,0:T(8,128)S(1)} all-reduce(f32[32,128]{1,0:T(8,128)S(1)} %rev.7), channel_id=1, replica_groups=mesh['row'=16,'col'=16] {'row'}, use_global_device_ids=true, to_apply=%region_3.0 | all-reduce | flops 4096 | bytes 32768 | tf_op jit(solution)/shard_map/psum | solution.py:91
  362.9 7.7 %convolution_convert_fusion.2 = bf16[256,512]{1,0:T(8,128)(2,1)} fusion(bf16[256,8192]{1,0:T(8,128)(2,1)} %all-gather.3.cloned.1.call-done, bf16[8192,512]{1,0:T(8,128)(2,1)} %all-gather.5.cloned.1.call-done), kind=kOutput, calls=%fused_computation.9 | convolution fusion | flops 2147614720 | bytes 12845056 | tf_op jit(solution)/shard_map/dot_general | solution.py:64
  370.6 20.6 %reduce-scatter.5.cloned.1.call-done = bf16[512,512]{1,0:T(8,128)(2,1)} async-done(((bf16[8192,512]{1,0:T(8,128)(2,1)}), bf16[512,512]{1,0:T(8,128)(2,1)}) %reduce-scatter.5.cloned.1.call-update) | async-done | bytes 524304 | tf_op jit(solution)/shard_map/reduce_scatter | solution.py:92
  391.2 1.9 multiply_convert_fusion
  (62 shorter events, 7.3 us)
Async XLA Ops:
  7.2 83.1 %copy-start = (bf16[256,512]{1,0:T(8,128)(2,1)S(1)}, bf16[256,512]{1,0:T(8,128)(2,1)}, u32[]{:S(2)}) copy-start(bf16[256,512]{1,0:T(8,128)(2,1)} %param.11) | copy-start | bytes 786436
  7.2 83.1 %all-gather.5.cloned.1.call-start = ((), (), s32[]{:S(2)}) async-start(), calls=%async_computation.3 | async-start | bytes 8912896 | tf_op jit(solution)/shard_map/all_gather | solution.py:63
  7.9 171.2 %reduce-scatter.3.cloned.1.call-start = ((), (), s32[]{:S(2)}) async-start(), calls=%async_computation.4 | async-start | bytes 4456448 | tf_op jit(solution)/shard_map/reduce_scatter | solution.py:69
  98.0 0.9 copy-start.6
  98.1 3.2 copy-start.7
  98.1 5.7 %copy-start.8 = (f32[32,128]{1,0:T(8,128)S(1)}, f32[32,128]{1,0:T(8,128)}, u32[]{:S(2)}) copy-start(f32[32,128]{1,0:T(8,128)} %param.9) | copy-start | bytes 49156
  98.1 177.3 %all-gather.3.cloned.1.call-start = ((), (), s32[]{:S(2)}) async-start(), calls=%async_computation.2 | async-start | bytes 4456448 | tf_op jit(solution)/shard_map/all_gather | solution.py:62
  99.2 83.8 %collective-permute-start = (bf16[128,512]{0,1:T(8,128)(2,1)S(1)}, bf16[128,512]{0,1:T(8,128)(2,1)S(1)}, u32[]{:S(2)}, u32[]{:S(2)}) collective-permute-start(bf16[128,512]{0,1:T(8,128)(2,1)S(1)} %slice.34), channel_id=1, source_target_pairs={{0,16},{16,32},{32,48},{48,64},{64,80},{80,96},{96,112},{112,128},... | collective-permute-start | bytes 393224 | tf_op jit(solution)/shard_map/ppermute | solution.py:11
  101.5 81.5 %collective-permute-start.1 = (bf16[128,512]{0,1:T(8,128)(2,1)S(1)}, bf16[128,512]{0,1:T(8,128)(2,1)S(1)}, u32[]{:S(2)}, u32[]{:S(2)}) collective-permute-start(bf16[128,512]{0,1:T(8,128)(2,1)S(1)} %slice.35), channel_id=1, source_target_pairs={{0,16},{16,32},{32,48},{48,64},{64,80},{80,96},{96,112},{112,128},... | collective-permute-start | bytes 393224 | tf_op jit(solution)/shard_map/ppermute | solution.py:11
  113.7 2.2 slice-start
  129.2 2.2 slice-start.1
  131.4 47.7 %copy-start.2 = (bf16[256,512]{1,0:T(8,128)(2,1)S(1)}, bf16[256,512]{1,0:T(8,128)(2,1)}, u32[]{:S(2)}) copy-start(bf16[256,512]{1,0:T(8,128)(2,1)} %param.6) | copy-start | bytes 786436
  180.8 4.7 %collective-permute-start.2 = (bf16[128,512]{1,0:T(8,128)(2,1)}, bf16[128,512]{1,0:T(8,128)(2,1)S(1)}, u32[]{:S(2)}, u32[]{:S(2)}) collective-permute-start(bf16[128,512]{1,0:T(8,128)(2,1)} %slice.42), channel_id=1, source_target_pairs={{16,0},{32,16},{48,32},{64,48},{80,64},{96,80},{112,96},{128,112},... | collective-permute-start | bytes 393224 | tf_op jit(solution)/shard_map/ppermute | solution.py:11
  194.0 6.5 %copy-start.3 = (bf16[256,512]{1,0:T(8,128)(2,1)S(1)}, bf16[256,512]{1,0:T(8,128)(2,1)}, u32[]{:S(2)}) copy-start(bf16[256,512]{1,0:T(8,128)(2,1)} %reduce-scatter.3.cloned.1.call-done) | copy-start | bytes 786436
  201.4 189.7 %reduce-scatter.5.cloned.1.call-start = ((), (), s32[]{:S(2)}) async-start(), calls=%async_computation.5 | async-start | bytes 8912896 | tf_op jit(solution)/shard_map/reduce_scatter | solution.py:92
  291.5 11.5 %copy-start.5 = (bf16[256,512]{0,1:T(8,128)(2,1)S(1)}, bf16[256,512]{0,1:T(8,128)(2,1)}, u32[]{:S(2)}) copy-start(bf16[256,512]{0,1:T(8,128)(2,1)} %get-tuple-element.13) | copy-start | bytes 786436
  291.5 12.4 %copy-start.4 = (bf16[256,512]{0,1:T(8,128)(2,1)S(1)}, bf16[256,512]{0,1:T(8,128)(2,1)}, u32[]{:S(2)}) copy-start(bf16[256,512]{0,1:T(8,128)(2,1)} %get-tuple-element.12) | copy-start | bytes 786436
  362.9 30.2 %copy-start.1 = (bf16[256,512]{1,0:T(8,128)(2,1)S(1)}, bf16[256,512]{1,0:T(8,128)(2,1)}, u32[]{:S(2)}) copy-start(bf16[256,512]{1,0:T(8,128)(2,1)} %param.11) | copy-start | bytes 786436
Sparse Core Ops, SparseCore 0:
  10.7 79.5 all-gather.4
  98.2 80.8 reduce-scatter.2
  201.6 73.8 all-gather.2
  283.4 107.7 reduce-scatter.4
where the time goes:
time: 400 us
  waiting for transfers between devices  224 us (56%)
  blocking collectives  57.5 us (14%)
  local copies, waits for them, and re-layouts  49.8 us (12%)
  matrix products  38.7 us (10%)
  between operations  14.1 us (4%)
  other arithmetic  8.78 us (2%)
  starting transfers between devices  6.92 us (2%)
    all_gather x1, waiting for transfers between devices, shards(): weights = lax.all_gather(out_weight, 'row', axis=0, tiled=True)  82.3 us
    all_gather x1, waiting for transfers between devices, shards(): panel = lax.all_gather(gated, 'col', axis=1, tiled=True)  73.7 us
    psum x1, blocking collectives, shards(): lax.psum(local_taps, 'row') * (1.0 / math.sqrt(total_tokens * group))  57.5 us
    reduce_scatter x1, waiting for transfers between devices, shards(): lax.psum_scatter(partial_value.astype(jnp.bfloat16), 'col', scatter_dimen...  44.5 us
    reduce_scatter x1, waiting for transfers between devices, shards(): lax.psum_scatter(lax.dot_general(panel, out_grad, (((0,), (0,)), ((), ())...  20.6 us
    another operation x4, local copies, waits for them, and re-layouts, toeplitz(): tiled = jnp.tile(template, (1, span))  19.6 us
    unnamed x27, local copies, waits for them, and re-layouts  12 us
    dot_general x2, matrix products, convolve(): jnp.einsum('gts,bsgc->btgc', matrix, split, precision=lax.Precision.HIGHEST)  11.9 us
  transfers between devices with their start and end apart: 7, of which 5 were waited for; matrix products, arithmetic and copies ran while one was open for 15% of the time, Pallas kernels for 0%

commit v1 on v0

--- a/solution.py
+++ b/solution.py
@@ -88,7 +88,9 @@
     )
     skewed = flat.reshape(groups, span, 2 * span + 1)[:, :, 1 : span + 1]
     local_taps = jnp.sum(skewed, axis=1)[:, ::-1]
-    filter_grad = lax.psum(local_taps, "row") * (1.0 / math.sqrt(total_tokens * group))
+    filter_grad = jnp.sum(lax.all_gather(local_taps, "row"), axis=0) * (
+        1.0 / math.sqrt(total_tokens * group)
+    )
     weight_sum = lax.psum_scatter(
         lax.dot_general(
             panel, out_grad, (((0,), (0,)), ((), ())), preferred_element_type=f32

time: 400 us -> 400 us (level)
  blocking collectives: 57.5 us -> 22.3 us
  waiting for transfers between devices: 224 us -> 258 us
    psum x1 -> x0, blocking collectives: 57.5 us -> none  [shards(): lax.psum(local_taps, 'row') * (1.0 / math.sqrt(total_tokens * group))]
    reduce_scatter x1, waiting for transfers between devices: 20.6 us -> 55.2 us  [shards(): lax.psum_scatter(lax.dot_general(panel, out_grad, (((0,), (0,)), ((), ())...]
    all_gather x0 -> x1, blocking collectives: none -> 22.3 us  [shards(): lax.all_gather(local_taps, 'row')]
where the time goes in v1:
time: 400 us; the launch traced here: 399 us
  waiting for transfers between devices  258 us (64%)
  local copies, waits for them, and re-layouts  49.8 us (12%)
  matrix products  38.7 us (10%)
  blocking collectives  22.3 us (6%)
  between operations  14.1 us (4%)
  other arithmetic  8.8 us (2%)
  starting transfers between devices  6.92 us (2%)
    all_gather x1, waiting for transfers between devices, shards(): weights = lax.all_gather(out_weight, 'row', axis=0, tiled=True)  82.3 us
    all_gather x1, waiting for transfers between devices, shards(): panel = lax.all_gather(gated, 'col', axis=1, tiled=True)  73.7 us
    reduce_scatter x1, waiting for transfers between devices, shards(): lax.psum_scatter(lax.dot_general(panel, out_grad, (((0,), (0,)), ((), ())...  55.2 us
    reduce_scatter x1, waiting for transfers between devices, shards(): lax.psum_scatter(partial_value.astype(jnp.bfloat16), 'col', scatter_dimen...  44.5 us
    all_gather x1, blocking collectives, shards(): lax.all_gather(local_taps, 'row')  22.3 us
    another operation x4, local copies, waits for them, and re-layouts, toeplitz(): tiled = jnp.tile(template, (1, span))  19.6 us
    unnamed x27, local copies, waits for them, and re-layouts  12 us
    dot_general x2, matrix products, convolve(): jnp.einsum('gts,bsgc->btgc', matrix, split, precision=lax.Precision.HIGHEST)  11.9 us
  transfers between devices with their start and end apart: 7, of which 5 were waited for; matrix products, arithmetic and copies ran while one was open for 15% of the time, Pallas kernels for 0%

profile of v1, /device:TPU:2, one launch (start us, length us, event | category | flops | bytes accessed | tf_op | source)
XLA Modules:
  0.0 399.1 jit_solution(13915365461820113868)
XLA Ops:
  8.0 82.3 %all-gather.6.cloned.1.call-done = bf16[8192,512]{1,0:T(8,128)(2,1)} async-done(((bf16[512,512]{1,0:T(8,128)(2,1)}), bf16[8192,512]{1,0:T(8,128)(2,1)}) %all-gather.6.cloned.1.call-update) | async-done | bytes 8388624 | tf_op jit(solution)/shard_map/all_gather | solution.py:63
  90.2 7.8 %convolution_convert_fusion.1 = bf16[256,8192]{1,0:T(8,128)(2,1)} fusion(bf16[256,512]{1,0:T(8,128)(2,1)S(1)} %copy-done, bf16[8192,512]{1,0:T(8,128)(2,1)} %all-gather.6.cloned.1.call-done), kind=kOutput, calls=%fused_computation.1 | convolution fusion | flops 2149580800 | bytes 12845056 | tf_op jit(solution)/shard_map/dot_general | solution.py:65
  98.1 0.9 copy-done.6
  99.2 2.1 collective-permute-start
  101.5 2.3 collective-permute-start.1
  103.9 3.1 tile.20
  107.0 6.7 %tile.21 = f32[32,32896]{1,0:T(8,128)} reshape(f32[32,128,257]{2,1,0:T(8,128)} %tile.20) | data formatting | bytes 8421376 | tf_op jit(solution)/shard_map/tile | solution.py:27
  113.7 2.2 slice-done
  115.9 3.3 copy.54
  119.4 3.1 tile.8
  122.5 6.7 %tile.9 = f32[32,32896]{1,0:T(8,128)} reshape(f32[32,128,257]{2,1,0:T(8,128)} %tile.8) | data formatting | bytes 8421376 | tf_op jit(solution)/shard_map/tile | solution.py:27
  129.2 2.2 slice-done.1
  131.4 3.2 copy.52
  134.6 44.5 %reduce-scatter.3.cloned.1.call-done = bf16[256,512]{1,0:T(8,128)(2,1)} async-done(((bf16[256,8192]{1,0:T(8,128)(2,1)}), bf16[256,512]{1,0:T(8,128)(2,1)}) %reduce-scatter.3.cloned.1.call-update) | async-done | bytes 262160 | tf_op jit(solution)/shard_map/reduce_scatter | solution.py:69
  179.1 1.0 convert_multiply_fusion
  180.8 2.1 collective-permute-start.2
  183.5 2.0 collective-permute-done.2
  186.2 5.9 %fusion.7 = f32[2,128,32,16]{1,3,0,2:T(8,128)S(1)} fusion(f32[32,128,256,1]{2,1,0,3:T(8,128)} %bitcast.61, f32[2,128,32,16]{1,3,0,2:T(8,128)S(1)} %copy.44, f32[2,128,32,16]{1,3,0,2:T(8,128)S(1)} %copy.43), kind=kOutput, calls=%fused_computation.8 | convolution fusion | flops 402915328 | bytes 5767168 | tf_op jit(solution)/shard_map/gts,bsgc->btgc/dot_general | solution.py:42
  192.4 0.9 fusion.14
  194.0 5.9 %fusion.4 = f32[2,128,32,16]{1,3,0,2:T(8,128)S(1)} fusion(f32[2,256,32,16]{1,3,0,2:T(8,128)S(1)} %copy_dynamic-update-slice_fusion, f32[32,128,256,1]{2,1,0,3:T(8,128)} %bitcast.60), kind=kOutput, calls=%fused_computation.7 | convolution fusion | flops 402653184 | bytes 5767168 | tf_op jit(solution)/shard_map/gts,bsgc->btgc/dot_general | solution.py:42
  200.5 0.9 fusion.16
  201.7 73.7 %all-gather.4.cloned.1.call-done = bf16[256,8192]{1,0:T(8,128)(2,1)} async-done(((bf16[256,512]{1,0:T(8,128)(2,1)}), bf16[256,8192]{1,0:T(8,128)(2,1)}) %all-gather.4.cloned.1.call-update) | async-done | bytes 4194320 | tf_op jit(solution)/shard_map/all_gather | solution.py:62
  275.4 7.8 %convolution_convert_fusion = bf16[8192,512]{1,0:T(8,128)(2,1)} fusion(bf16[256,8192]{1,0:T(8,128)(2,1)} %all-gather.4.cloned.1.call-done, bf16[256,512]{1,0:T(8,128)(2,1)S(1)} %copy-done), kind=kOutput, calls=%fused_computation | convolution fusion | flops 2151677952 | bytes 12845056 | tf_op jit(solution)/shard_map/dot_general | solution.py:95
  283.2 3.5 fusion.18
  286.7 2.4 copy.56
  289.2 2.3 concatenate.42
  291.5 8.2 %reshape.61 = f32[32,128,257]{2,1,0:T(8,128)} reshape(f32[32,32896]{1,0:T(8,128)} %concatenate.42) | data formatting | bytes 8421376 | tf_op jit(solution)/shard_map/reshape | solution.py:89
  299.7 3.2 slice_reduce_fusion
  303.0 22.3 %all-gather = f32[512,128]{1,0:T(8,128)S(1)} all-gather(f32[32,128]{1,0:T(8,128)S(1)} %rev.7), channel_id=2, replica_groups=mesh['row'=16,'col'=16] {'row'}, dimensions={0}, use_global_device_ids=true | all-gather | bytes 278528 | tf_op jit(solution)/shard_map/all_gather | solution.py:91
  327.7 7.8 %convolution_convert_fusion.2 = bf16[256,512]{1,0:T(8,128)(2,1)} fusion(bf16[256,8192]{1,0:T(8,128)(2,1)} %all-gather.4.cloned.1.call-done, bf16[8192,512]{1,0:T(8,128)(2,1)} %all-gather.6.cloned.1.call-done), kind=kOutput, calls=%fused_computation.9 | convolution fusion | flops 2147614720 | bytes 12845056 | tf_op jit(solution)/shard_map/dot_general | solution.py:64
  335.5 55.2 %reduce-scatter.5.cloned.1.call-done = bf16[512,512]{1,0:T(8,128)(2,1)} async-done(((bf16[8192,512]{1,0:T(8,128)(2,1)}), bf16[512,512]{1,0:T(8,128)(2,1)}) %reduce-scatter.5.cloned.1.call-update) | async-done | bytes 524304 | tf_op jit(solution)/shard_map/reduce_scatter | solution.py:94
  390.7 1.9 multiply_convert_fusion
  (63 shorter events, 7.3 us)
Async XLA Ops:
  7.2 83.1 %copy-start = (bf16[256,512]{1,0:T(8,128)(2,1)S(1)}, bf16[256,512]{1,0:T(8,128)(2,1)}, u32[]{:S(2)}) copy-start(bf16[256,512]{1,0:T(8,128)(2,1)} %param.11) | copy-start | bytes 786436
  7.2 83.1 %all-gather.6.cloned.1.call-start = ((), (), s32[]{:S(2)}) async-start(), calls=%async_computation.3 | async-start | bytes 8912896 | tf_op jit(solution)/shard_map/all_gather | solution.py:63
  7.9 171.2 %reduce-scatter.3.cloned.1.call-start = ((), (), s32[]{:S(2)}) async-start(), calls=%async_computation.4 | async-start | bytes 4456448 | tf_op jit(solution)/shard_map/reduce_scatter | solution.py:69
  98.0 0.9 copy-start.6
  98.1 3.2 copy-start.7
  98.1 5.7 %copy-start.8 = (f32[32,128]{1,0:T(8,128)S(1)}, f32[32,128]{1,0:T(8,128)}, u32[]{:S(2)}) copy-start(f32[32,128]{1,0:T(8,128)} %param.9) | copy-start | bytes 49156
  98.1 177.3 %all-gather.4.cloned.1.call-start = ((), (), s32[]{:S(2)}) async-start(), calls=%async_computation.2 | async-start | bytes 4456448 | tf_op jit(solution)/shard_map/all_gather | solution.py:62
  99.2 83.8 %collective-permute-start = (bf16[128,512]{0,1:T(8,128)(2,1)S(1)}, bf16[128,512]{0,1:T(8,128)(2,1)S(1)}, u32[]{:S(2)}, u32[]{:S(2)}) collective-permute-start(bf16[128,512]{0,1:T(8,128)(2,1)S(1)} %slice.34), channel_id=1, source_target_pairs={{0,16},{16,32},{32,48},{48,64},{64,80},{80,96},{96,112},{112,128},... | collective-permute-start | bytes 393224 | tf_op jit(solution)/shard_map/ppermute | solution.py:11
  101.5 81.5 %collective-permute-start.1 = (bf16[128,512]{0,1:T(8,128)(2,1)S(1)}, bf16[128,512]{0,1:T(8,128)(2,1)S(1)}, u32[]{:S(2)}, u32[]{:S(2)}) collective-permute-start(bf16[128,512]{0,1:T(8,128)(2,1)S(1)} %slice.35), channel_id=1, source_target_pairs={{0,16},{16,32},{32,48},{48,64},{64,80},{80,96},{96,112},{112,128},... | collective-permute-start | bytes 393224 | tf_op jit(solution)/shard_map/ppermute | solution.py:11
  113.7 2.2 slice-start
  129.2 2.2 slice-start.1
  131.4 47.7 %copy-start.2 = (bf16[256,512]{1,0:T(8,128)(2,1)S(1)}, bf16[256,512]{1,0:T(8,128)(2,1)}, u32[]{:S(2)}) copy-start(bf16[256,512]{1,0:T(8,128)(2,1)} %param.6) | copy-start | bytes 786436
  180.8 4.7 %collective-permute-start.2 = (bf16[128,512]{1,0:T(8,128)(2,1)}, bf16[128,512]{1,0:T(8,128)(2,1)S(1)}, u32[]{:S(2)}, u32[]{:S(2)}) collective-permute-start(bf16[128,512]{1,0:T(8,128)(2,1)} %slice.42), channel_id=1, source_target_pairs={{16,0},{32,16},{48,32},{64,48},{80,64},{96,80},{112,96},{128,112},... | collective-permute-start | bytes 393224 | tf_op jit(solution)/shard_map/ppermute | solution.py:11
  194.0 6.5 %copy-start.3 = (bf16[256,512]{1,0:T(8,128)(2,1)S(1)}, bf16[256,512]{1,0:T(8,128)(2,1)}, u32[]{:S(2)}) copy-start(bf16[256,512]{1,0:T(8,128)(2,1)} %reduce-scatter.3.cloned.1.call-done) | copy-start | bytes 786436
  201.4 189.2 %reduce-scatter.5.cloned.1.call-start = ((), (), s32[]{:S(2)}) async-start(), calls=%async_computation.5 | async-start | bytes 8912896 | tf_op jit(solution)/shard_map/reduce_scatter | solution.py:94
  291.5 33.9 %copy-start.5 = (bf16[256,512]{0,1:T(8,128)(2,1)S(1)}, bf16[256,512]{0,1:T(8,128)(2,1)}, u32[]{:S(2)}) copy-start(bf16[256,512]{0,1:T(8,128)(2,1)} %get-tuple-element.19) | copy-start | bytes 786436
  291.5 34.7 %copy-start.4 = (bf16[256,512]{0,1:T(8,128)(2,1)S(1)}, bf16[256,512]{0,1:T(8,128)(2,1)}, u32[]{:S(2)}) copy-start(bf16[256,512]{0,1:T(8,128)(2,1)} %get-tuple-element.18) | copy-start | bytes 786436
  327.7 64.9 %copy-start.1 = (bf16[256,512]{1,0:T(8,128)(2,1)S(1)}, bf16[256,512]{1,0:T(8,128)(2,1)}, u32[]{:S(2)}) copy-start(bf16[256,512]{1,0:T(8,128)(2,1)} %param.11) | copy-start | bytes 786436
Sparse Core Ops, SparseCore 0:
  10.7 79.5 all-gather.5
  98.2 80.8 reduce-scatter.2
  201.6 73.8 all-gather.3
  283.4 107.2 reduce-scatter.4
